TPU v7x, 32 devices: a whole 2x2x4 slice. The times are simulated.
32 devices in a mesh: groups: 2 (over y), ctx: 4 (over z), mp: 4 (over x, core).
Axes of the slice: x: 2, y: 2, z: 4, core: 2. Of those that a mesh axis runs over, the one named last changes fastest.
Arguments:
- streams: bfloat16 [3, 2048, 4096], P(None, ('groups', 'ctx'), 'mp'), parts along dimension 1, may hold values from -6 to 6
- short_filter: float32 [3, 3, 4096], P(None, None, 'mp'), may hold values from -3 to 3
- mode_params: float32 [2, 4096, 8], P(None, 'mp'), may hold values from -2 to 2, as said below
- out_weight: bfloat16 [4096, 4096], P('mp', 'ctx'), may hold values from -0.09375 to 0.09375
- norm_gain: float32 [4096], P('mp'), may hold values from 0.5 to 1.5
- unembed: bfloat16 [4096, 512], P('mp'), may hold values from -40 to 40
- native: int32 [2048], P(('groups', 'ctx')), parts along dimension 0, may hold values from 0 to 511
- mut_pos: int32 [512], P('groups'), parts along dimension 0, may hold values from 0 to 1023
- mut_ids: int32 [512], P('groups'), parts along dimension 0, may hold values from 0 to 511
Outputs:
- loglik: float32 [2048], P(('groups', 'ctx')), parts along dimension 0
- scores: float32 [512], P('groups'), parts along dimension 0
There are 2 independent parts, one for each index of `groups`. A program takes and returns all parts, laid end to end along the dimension named above; an argument that names none is the same for every part. Nothing has to cross between parts.
Inputs may be any that keep to these rules, and one draw needn't show every extreme that they name: mode_params[0] holds positive decay rates, mode_params[1] residues.
All inputs are finite; a program needn't handle non-finite values.
Results may differ from a plain program's by a relative error of at most 0.0065.
Values may be sent and summed in bfloat16 or wider, within the bound.
No kernel may reach another device: no remote copies, remote signals or barrier semaphores. Data moves between devices by JAX's collectives and lax.ppermute only.
A program may use at most 192 MiB of HBM per device.

v0:
```python
import jax
import jax.numpy as jnp
from jax import lax
from jax.sharding import PartitionSpec as P

D = 4096
PRECISE = lax.Precision.HIGHEST


def from_behind(value, axis, steps):
    count = lax.axis_size(axis)
    initial, last = (max(0, -steps), min(count, count - steps))
    return lax.ppermute(value, axis, [(source, source + steps) for source in range(initial, last)])


def prefix(value, axis, join, neutral):
    count, mine = (lax.axis_size(axis), lax.axis_index(axis))
    pieces = jax.tree.map(lambda part: lax.all_gather(part, axis), value)
    so_far = jax.tree.map(
        lambda part, zero: jnp.full_like(part, 0) + jnp.asarray(zero, part.dtype), value, neutral
    )

    def hop(position, so_far):
        longer = join(so_far, jax.tree.map(lambda part: part[position], pieces))
        return jax.tree.map(lambda new, old: jnp.where(position < mine, new, old), longer, so_far)

    return lax.fori_loop(0, count - 1, hop, so_far)


def short_mix(padded, short_filter, seq_rows):
    return (
        short_filter[:, 0, None, :] * padded[:, 2:, :]
        + short_filter[:, 1, None, :] * padded[:, 1 : seq_rows + 1, :]
        + short_filter[:, 2, None, :] * padded[:, 0:seq_rows, :]
    )


def carry_terms(starts, decays, residue, span_len):
    lag_steps = jnp.arange(span_len, dtype=jnp.float32)
    weights = residue[None] * jnp.exp(-decays[None] * (lag_steps + 1.0)[:, None, None])
    return jnp.einsum("ncm,tcm->ntc", starts, weights, precision=PRECISE)


def span_conv(values, decays, residue, span_len):
    seq_all, channels = values.shape
    spans = seq_all // span_len
    lag_steps = jnp.arange(span_len, dtype=jnp.float32)
    powers = jnp.exp(-decays[None] * lag_steps[:, None, None])
    kernel = jnp.sum(residue[None] * powers, axis=2)
    offsets = jnp.arange(span_len, dtype=jnp.int32)
    spread = offsets[:, None] - offsets[None, :]
    toeplitz = jnp.where((spread >= 0)[:, :, None], kernel[jnp.clip(spread, 0, span_len - 1)], 0.0)
    blocked = values.reshape(spans, span_len, channels)
    inside = jnp.einsum("tsc,nsc->ntc", toeplitz, blocked, precision=PRECISE)
    tail_pows = jnp.exp(-decays[None] * (span_len - 1.0 - lag_steps)[:, None, None])
    own_states = jnp.einsum("nsc,scm->ncm", blocked, tail_pows, precision=PRECISE)
    factor = jnp.exp(-decays * span_len)

    def advance(carried, own_part):
        return (factor * carried + own_part, carried)

    end_state, starts = lax.scan(advance, jnp.zeros_like(factor), own_states)
    result = inside + carry_terms(starts, decays, residue, span_len)
    return (result.reshape(seq_all, channels), end_state)


def enter_terms(entering, decays, residue, spans, span_len):
    span_index = jnp.arange(spans, dtype=jnp.float32)
    starts = jnp.exp(-decays[None] * (span_index * span_len)[:, None, None]) * entering[None]
    added = carry_terms(starts, decays, residue, span_len)
    return added.reshape(spans * span_len, decays.shape[0])


def chain_pair(earlier, following):
    return (earlier[0] * following[0], following[0] * earlier[1] + following[1])


def body(
    streams, short_filter, mode_params, out_weight, norm_gain, unembed, native, mut_pos, mut_ids
):
    seq_rows = streams.shape[1]
    prior = from_behind(streams[:, seq_rows - 2 :, :], "ctx", 1)
    padded = jnp.concatenate([prior, streams], axis=1).astype(jnp.float32)
    mixed = short_mix(padded, short_filter, seq_rows)
    gate_bf = lax.optimization_barrier(mixed[0].astype(jnp.bfloat16))
    product = (mixed[1] * mixed[2]).astype(jnp.bfloat16)
    decays = mode_params[0]
    residue = mode_params[1]
    span_len = min(64, seq_rows)
    spans = seq_rows // span_len
    inside, own_end = span_conv(product.astype(jnp.float32), decays, residue, span_len)
    factor = jnp.exp(-decays * seq_rows)
    unused, entering = prefix(
        (factor, own_end), "ctx", chain_pair, (jnp.ones_like(factor), jnp.zeros_like(own_end))
    )
    conv_sum = inside + enter_terms(entering, decays, residue, spans, span_len)
    conv_bf = conv_sum.astype(jnp.bfloat16)
    conv_bf = lax.optimization_barrier(conv_bf)
    gated = (gate_bf.astype(jnp.float32) * conv_bf.astype(jnp.float32)).astype(jnp.bfloat16)
    terms = jnp.dot(
        gated,
        lax.all_gather(out_weight, "ctx", axis=1, tiled=True),
        preferred_element_type=jnp.float32,
    )
    output = lax.psum_scatter(terms, "mp", scatter_dimension=1, tiled=True)
    squares = lax.psum(jnp.sum(output * output, axis=1), "mp")
    normed = (output * lax.rsqrt(squares[:, None] / D + 1e-05) * norm_gain).astype(jnp.bfloat16)
    logit_terms = jnp.dot(normed, unembed, preferred_element_type=jnp.float32)
    local_pos = mut_pos - lax.axis_index("ctx") * seq_rows
    owned_mut = (local_pos >= 0) & (local_pos < seq_rows)
    slot_rows = jnp.clip(local_pos, 0, seq_rows - 1)
    logits = lax.psum(logit_terms, "mp")
    vocab_ids = jnp.arange(logits.shape[1], dtype=jnp.int32)
    totals = jax.nn.logsumexp(logits, axis=1)
    picked = jnp.sum(jnp.where(vocab_ids[None, :] == native[:, None], logits, 0.0), axis=1)
    chosen = jnp.sum(
        jnp.where(vocab_ids[None, :] == mut_ids[:, None], logits[slot_rows], 0.0), axis=1
    )
    loglik = picked - totals
    mut_terms = jnp.where(owned_mut, chosen - picked[slot_rows], 0.0)
    scores = lax.psum(mut_terms, "ctx")
    return (loglik, scores)


def solution(mesh):
    in_specs = (
        P(None, ("groups", "ctx"), "mp"),
        P(None, None, "mp"),
        P(None, "mp", None),
        P("mp", "ctx"),
        P("mp"),
        P("mp", None),
        P(("groups", "ctx")),
        P("groups"),
        P("groups"),
    )
    out_specs = (P(("groups", "ctx")), P("groups"))
    return jax.shard_map(body, mesh=mesh, in_specs=in_specs, out_specs=out_specs, check_vma=False)
```

profile of v0, /device:TPU:0, one launch (start us, length us, event | category | flops | bytes accessed | tf_op | source)
XLA Modules:
  0.0 301.2 jit_solution(9533523569857050880)
XLA Ops:
  8.8 5.0 %collective-permute-start = (bf16[3,2,1024]{2,1,0:T(2,128)(2,1)S(1)}, bf16[3,2,1024]{2,1,0:T(2,128)(2,1)S(1)}, u32[]{:S(2)}, u32[]{:S(2)}) collective-permute-start(bf16[3,2,1024]{2,1,0:T(2,128)(2,1)S(1)} %slice.38), channel_id=1, source_target_pairs={{0,4},{4,8},{8,12},{1,5},{5,9},{9,13},{2,6},{6,10},{10,14},{3,7},{... | collective-permute-start | bytes 36872 | tf_op jit(solution)/shard_map/ppermute | solution.py:13
  15.2 5.8 %multiply_reduce_fusion = f32[64,1024]{0,1:T(8,128)S(1)} fusion(f32[1024,8]{1,0:T(8,128)S(1)} %copy.32, f32[1024,8]{1,0:T(8,128)S(1)} %copy.31), kind=kLoop, calls=%fused_computation.18 | loop fusion | flops 1507328 | bytes 327680 | tf_op jit(solution)/shard_map/reduce_sum | solution.py:49
  21.0 20.9 %all_gather.13 = f32[4,1024,8]{1,2,0:T(8,128)S(1)} all-gather(f32[1,1024,8]{1,2,0:T(8,128)S(1)} %get-tuple-element.201), channel_id=1, replica_groups=mesh['groups'=2,'ctx'=4,'mp'=4] {'ctx'}, dimensions={0}, use_global_device_ids=true | all-gather | bytes 163840 | tf_op jit(solution)/shard_map/all_gather | solution.py:18
  42.1 18.4 %gather_fusion = f32[4096,1024]{1,0:T(8,128)} fusion(f32[64,1024]{1,0:T(8,128)S(1)} %copy.33, s32[4096]{0:T(1024)S(1)} %broadcast_clamp_fusion), kind=kCustom, calls=%fused_computation | custom fusion | bytes 33570816 | tf_op jit(solution)/shard_map/gather | solution.py:52
  60.6 30.5 %copy.34 = f32[64,64,1024]{1,0,2:T(8,128)} copy(f32[64,64,1024]{2,1,0:T(8,128)} %bitcast.58) | data formatting | bytes 33554432 | tf_op jit(solution)/shard_map/gather | solution.py:52
  91.1 1.9 maximum_convert_fusion
  93.9 1.6 copy-done.2
  96.4 6.0 %fusion.26 = f32[4,1024,8]{2,0,1:T(4,128)} fusion(bf16[4,64,1024]{1,0,2:T(4,128)(2,1)S(1)} %copy.35, f32[64]{0:T(128)S(1)} %iota_subtract_fusion, f32[1024,8]{1,0:T(8,128)S(1)} %copy.32), kind=kOutput, calls=%fused_computation.38 | convolution fusion | flops 25690112 | bytes 688384 | tf_op jit(solution)/shard_map/nsc,scm->ncm/dot_general | solution.py:56
  102.4 1.9 copy.37
  104.3 2.5 while.27
  106.9 15.5 %all-gather = f32[4096,8]{0,1:T(8,128)S(1)} all-gather(f32[1024,8]{0,1:T(8,128)S(1)} %get-tuple-element.125), channel_id=2, replica_groups=mesh['groups'=2,'ctx'=4,'mp'=4] {'ctx'}, dimensions={0}, use_global_device_ids=true | all-gather | bytes 163840 | tf_op jit(solution)/shard_map/all_gather | solution.py:18
  123.5 2.5 copy.38
  126.0 10.4 %fusion.8 = f32[1024,64,4]{1,2,0:T(4,128)S(1)} fusion(f32[64]{0:T(128)S(1)} %iota_add_fusion, f32[1024,8]{1,0:T(8,128)S(1)} %copy.32, f32[1024,8]{1,0:T(8,128)S(1)} %copy-done.4, f32[1024,8]{1,0:T(8,128)} %copy.40, f32[4]{0:T(128)S(1)} %iota_multiply_fusion), kind=kOutput, calls=%fused_computation.16 | convolution fusion | flops 26279936 | bytes 1147152 | tf_op jit(solution)/shard_map/ncm,tcm->ntc/dot_general | solution.py:41
  136.5 9.8 %fusion.9 = f32[1024,64,4]{1,2,0:T(4,128)S(1)} fusion(f32[4,1024,8]{2,0,1:T(4,128)S(1)} %copy-done.5, f32[64]{0:T(128)S(1)} %iota_add_fusion, f32[1024,8]{1,0:T(8,128)S(1)} %copy.32, f32[1024,8]{1,0:T(8,128)S(1)} %copy-done.4), kind=kOutput, calls=%fused_computation.17 | convolution fusion | flops 26214400 | bytes 1245440 | tf_op jit(solution)/shard_map/ncm,tcm->ntc/dot_general | solution.py:41
  146.2 29.9 %fusion.12 = bf16[4,64,1024]{1,0,2:T(4,128)(2,1)S(1)} fusion(f32[1024,64,4]{1,2,0:T(4,128)S(1)} %fusion.8, f32[1024,64,4]{1,2,0:T(4,128)S(1)} %fusion.9, bf16[4,64,1024]{1,0,2:T(4,128)(2,1)S(1)} %copy.35, f32[64,64,1024]{1,0,2:T(8,128)} %copy.34, pred[64,64]{1,0:T(8,128)(4,1)S(1)} %subtract_compare_fusion), kind=kOutput, calls=%fused_computation.25 | convolution fusion | flops 206307328 | bytes 19927040 | tf_op jit(solution)/shard_map/tsc,nsc->ntc/dot_general | solution.py:54
  178.1 7.6 %fusion.33 = f32[256,4096]{1,0:T(8,128)} fusion(bf16[1024,4096]{1,0:T(8,128)(2,1)} %all-gather.3.cloned.1.call-done, bf16[256,1024]{1,0:T(8,128)(2,1)S(1)} %bitcast.59, bf16[256,1024]{1,0:T(8,128)(2,1)S(1)} %fusion.35), kind=kOutput, calls=%fused_computation.49 | convolution fusion | flops 2148532224 | bytes 13631488 | tf_op jit(solution)/shard_map/dot_general | solution.py:100
  185.8 46.4 %reduce-scatter.2.cloned.1.call-done = f32[256,1024]{1,0:T(8,128)} async-done(((f32[256,4096]{1,0:T(8,128)}), f32[256,1024]{1,0:T(8,128)}) %reduce-scatter.2.cloned.1.call-update) | async-done | bytes 1048592 | tf_op jit(solution)/shard_map/reduce_scatter | solution.py:105
  232.2 1.4 multiply_reduce_fusion.1
  233.6 5.8 %psum.21 = f32[256]{0:T(256)S(1)} all-reduce(f32[256]{0:T(256)S(1)} %multiply_reduce_fusion.1), channel_id=1, replica_groups=mesh['groups'=2,'ctx'=4,'mp'=4] {'mp'}, use_global_device_ids=true, to_apply=%region_7.8 | all-reduce | flops 256 | bytes 2048 | tf_op jit(solution)/shard_map/psum | solution.py:106
  239.4 2.5 fusion.34
  242.0 34.1 %all-reduce.2.cloned.1.call-done = f32[256,512]{1,0:T(8,128)} async-done(((f32[256,512]{1,0:T(8,128)}), f32[256,512]{1,0:T(8,128)}) %all-reduce.2.cloned.1.call-update) | async-done | bytes 524304 | tf_op jit(solution)/shard_map/psum | solution.py:112
  277.4 1.3 exponential_reduce_fusion
  278.7 1.9 gather_fusion.2
  281.9 12.2 %psum.23 = f32[256]{0:T(256)} all-reduce(f32[256]{0:T(256)S(1)} %and_select_fusion), channel_id=1, replica_groups=mesh['groups'=2,'ctx'=4,'mp'=4] {'ctx'}, use_global_device_ids=true, to_apply=%region_13.14 | all-reduce | flops 256 | bytes 2048 | tf_op jit(solution)/shard_map/psum | solution.py:121
  (74 shorter events, 13.6 us)
Async XLA Ops:
  7.2 232.2 %copy-start = (bf16[1024,512]{1,0:T(8,128)(2,1)S(1)}, bf16[1024,512]{1,0:T(8,128)(2,1)}, u32[]{:S(2)}) copy-start(bf16[1024,512]{1,0:T(8,128)(2,1)} %param.18) | copy-start | bytes 3145732
  7.2 7.9 %copy-start.6 = (f32[3,3,1024]{2,1,0:T(4,128)S(1)}, f32[3,3,1024]{2,1,0:T(4,128)}, u32[]{:S(2)}) copy-start(f32[3,3,1024]{2,1,0:T(4,128)} %param.14) | copy-start | bytes 110596
  7.2 170.9 %all-gather.3.cloned.1.call-start = ((), (), s32[]{:S(2)}) async-start(), calls=%async_computation.1 | async-start | bytes 10485760 | tf_op jit(solution)/shard_map/all_gather | solution.py:102
  7.9 224.3 %reduce-scatter.2.cloned.1.call-start = ((), (), s32[]{:S(2)}) async-start(), calls=%async_computation.2 | async-start | bytes 5242880 | tf_op jit(solution)/shard_map/reduce_scatter | solution.py:105
  8.8 82.3 %collective-permute-start = (bf16[3,2,1024]{2,1,0:T(2,128)(2,1)S(1)}, bf16[3,2,1024]{2,1,0:T(2,128)(2,1)S(1)}, u32[]{:S(2)}, u32[]{:S(2)}) collective-permute-start(bf16[3,2,1024]{2,1,0:T(2,128)(2,1)S(1)} %slice.38), channel_id=1, source_target_pairs={{0,4},{4,8},{8,12},{1,5},{5,9},{9,13},{2,6},{6,10},{10,14},{3,7},{... | collective-permute-start | bytes 36872 | tf_op jit(solution)/shard_map/ppermute | solution.py:13
  15.0 27.0 %copy-start.3 = (f32[1024,8]{1,0:T(8,128)}, f32[1024,8]{1,0:T(8,128)S(1)}, u32[]{:S(2)}) copy-start(f32[1024,8]{1,0:T(8,128)S(1)} %copy.31) | copy-start | bytes 98308
  93.9 1.6 copy-start.2
  102.4 23.6 %copy-start.4 = (f32[1024,8]{1,0:T(8,128)S(1)}, f32[1024,8]{1,0:T(8,128)}, u32[]{:S(2)}) copy-start(f32[1024,8]{1,0:T(8,128)} %copy-done.3) | copy-start | bytes 98308
  126.0 10.4 %copy-start.5 = (f32[4,1024,8]{2,0,1:T(4,128)S(1)}, f32[4,1024,8]{2,0,1:T(4,128)}, u32[]{:S(2)}) copy-start(f32[4,1024,8]{2,0,1:T(4,128)} %copy.38) | copy-start | bytes 393220
  185.7 53.7 %copy-start.7 = (f32[1024]{0:T(1024)S(1)}, f32[1024]{0:T(1024)}, u32[]{:S(2)}) copy-start(f32[1024]{0:T(1024)} %param.17) | copy-start | bytes 12292
  185.7 56.2 %copy-start.8 = (s32[256]{0:T(256)S(1)}, s32[256]{0:T(256)}, u32[]{:S(2)}) copy-start(s32[256]{0:T(256)} %param.20) | copy-start | bytes 3076
  185.8 91.6 %copy-start.9 = (s32[256]{0:T(256)S(1)}, s32[256]{0:T(256)}, u32[]{:S(2)}) copy-start(s32[256]{0:T(256)} %param.19) | copy-start | bytes 3076
  185.8 90.3 %all-reduce.2.cloned.1.call-start = ((), (), s32[]{:S(2)}) async-start(), calls=%async_computation.3 | async-start | bytes 1048576 | tf_op jit(solution)/shard_map/psum | solution.py:112
  276.1 4.6 %copy-start.1 = (f32[256,512]{1,0:T(8,128)S(1)}, f32[256,512]{1,0:T(8,128)}, u32[]{:S(2)}) copy-start(f32[256,512]{1,0:T(8,128)} %all-reduce.2.cloned.1.call-done) | copy-start | bytes 1572868
  277.4 4.3 %copy-start.10 = (s32[256]{0:T(256)S(1)}, s32[256]{0:T(256)}, u32[]{:S(2)}) copy-start(s32[256]{0:T(256)} %param.21) | copy-start | bytes 3076
Sparse Core Ops, SparseCore 0:
  9.6 156.0 all-gather.2
  185.9 46.3 reduce-scatter.1
  242.0 34.0 all-reduce.1
where the time goes:
time: 303 us; the launch traced here: 301 us
  waiting for transfers between devices  81.3 us (27%)
  matrix products  66.2 us (22%)
  local copies, waits for them, and re-layouts  63.1 us (21%)
  blocking collectives  54.4 us (18%)
  other arithmetic  16.9 us (6%)
  between operations  14.1 us (5%)
  starting transfers between devices  5.07 us (2%)
    gather x2, local copies, waits for them, and re-layouts, span_conv(): kernel[jnp.clip(spread, 0, span_len - 1)]  48.9 us
    reduce_scatter x1, waiting for transfers between devices, body(): output = lax.psum_scatter(terms, 'mp', scatter_dimension=1, tiled=True)  46.4 us
    all_gather x2, blocking collectives, prefix(): pieces = jax.tree.map(lambda part: lax.all_gather(part, axis), value)  36.4 us
    psum x1, waiting for transfers between devices, body(): logits = lax.psum(logit_terms, 'mp')  34.1 us
    dot_general x1, matrix products, span_conv(): inside = jnp.einsum('tsc,nsc->ntc', toeplitz, blocked, precision=PRECISE)  29.9 us
    dot_general x2, matrix products, carry_terms(): return jnp.einsum('ncm,tcm->ntc', starts, weights, precision=PRECISE)  20.2 us
    psum x1, blocking collectives, body(): scores = lax.psum(mut_terms, 'ctx')  12.2 us
    dot_general x1, matrix products, body(): jnp.dot(gated, lax.all_gather(out_weight, 'ctx', axis=1, tiled=True), pre...  7.64 us
  transfers between devices with their start and end apart: 4, of which 2 were waited for; matrix products, arithmetic and copies ran while one was open for 42% of the time, Pallas kernels for 0%

commit v1 on v0

--- a/solution.py
+++ b/solution.py
@@ -109,7 +109,7 @@
     local_pos = mut_pos - lax.axis_index("ctx") * seq_rows
     owned_mut = (local_pos >= 0) & (local_pos < seq_rows)
     slot_rows = jnp.clip(local_pos, 0, seq_rows - 1)
-    logits = lax.psum(logit_terms, "mp")
+    logits = jnp.sum(lax.all_gather(logit_terms, "mp"), axis=0)
     vocab_ids = jnp.arange(logits.shape[1], dtype=jnp.int32)
     totals = jax.nn.logsumexp(logits, axis=1)
     picked = jnp.sum(jnp.where(vocab_ids[None, :] == native[:, None], logits, 0.0), axis=1)

time: 303 us -> 291 us (0.960)
  waiting for transfers between devices: 81.3 us -> 70.5 us
    psum x1 -> x0, waiting for transfers between devices: 34.1 us -> none  [body(): logits = lax.psum(logit_terms, 'mp')]
    all_gather x0 -> x1, waiting for transfers between devices: none -> 23.3 us  [body(): logits = jnp.sum(lax.all_gather(logit_terms, 'mp'), axis=0)]
  transfers between devices with their start and end apart: 4 -> 4, of which waited for: 2 -> 2; matrix products, arithmetic and copies ran while one was open for 42% -> 44% of each run, Pallas kernels for 0% -> 0%
where the time goes in v1:
time: 291 us; the launch traced here: 290 us
  waiting for transfers between devices  70.5 us (24%)
  matrix products  66.2 us (23%)
  local copies, waits for them, and re-layouts  63.1 us (22%)
  blocking collectives  54.4 us (19%)
  other arithmetic  16.6 us (6%)
  between operations  14.1 us (5%)
  starting transfers between devices  5.07 us (2%)
    gather x2, local copies, waits for them, and re-layouts, span_conv(): kernel[jnp.clip(spread, 0, span_len - 1)]  48.9 us
    reduce_scatter x1, waiting for transfers between devices, body(): output = lax.psum_scatter(terms, 'mp', scatter_dimension=1, tiled=True)  46.4 us
    all_gather x2, blocking collectives, prefix(): pieces = jax.tree.map(lambda part: lax.all_gather(part, axis), value)  36.4 us
    dot_general x1, matrix products, span_conv(): inside = jnp.einsum('tsc,nsc->ntc', toeplitz, blocked, precision=PRECISE)  29.9 us
    all_gather x1, waiting for transfers between devices, body(): logits = jnp.sum(lax.all_gather(logit_terms, 'mp'), axis=0)  23.3 us
    dot_general x2, matrix products, carry_terms(): return jnp.einsum('ncm,tcm->ntc', starts, weights, precision=PRECISE)  20.2 us
    psum x1, blocking collectives, body(): scores = lax.psum(mut_terms, 'ctx')  12.2 us
    dot_general x1, matrix products, body(): jnp.dot(gated, lax.all_gather(out_weight, 'ctx', axis=1, tiled=True), pre...  7.64 us
  transfers between devices with their start and end apart: 4, of which 2 were waited for; matrix products, arithmetic and copies ran while one was open for 44% of the time, Pallas kernels for 0%

profile of v1, /device:TPU:0, one launch (start us, length us, event | category | flops | bytes accessed | tf_op | source)
XLA Modules:
  0.0 290.1 jit_solution(14660191212644134595)
XLA Ops:
  8.8 5.0 %collective-permute-start = (bf16[3,2,1024]{2,1,0:T(2,128)(2,1)S(1)}, bf16[3,2,1024]{2,1,0:T(2,128)(2,1)S(1)}, u32[]{:S(2)}, u32[]{:S(2)}) collective-permute-start(bf16[3,2,1024]{2,1,0:T(2,128)(2,1)S(1)} %slice.38), channel_id=1, source_target_pairs={{0,4},{4,8},{8,12},{1,5},{5,9},{9,13},{2,6},{6,10},{10,14},{3,7},{... | collective-permute-start | bytes 36872 | tf_op jit(solution)/shard_map/ppermute | solution.py:13
  15.2 5.8 %multiply_reduce_fusion = f32[64,1024]{0,1:T(8,128)S(1)} fusion(f32[1024,8]{1,0:T(8,128)S(1)} %copy.32, f32[1024,8]{1,0:T(8,128)S(1)} %copy.31), kind=kLoop, calls=%fused_computation.18 | loop fusion | flops 1507328 | bytes 327680 | tf_op jit(solution)/shard_map/reduce_sum | solution.py:49
  21.0 20.9 %all_gather.19 = f32[4,1024,8]{1,2,0:T(8,128)S(1)} all-gather(f32[1,1024,8]{1,2,0:T(8,128)S(1)} %get-tuple-element.201), channel_id=1, replica_groups=mesh['groups'=2,'ctx'=4,'mp'=4] {'ctx'}, dimensions={0}, use_global_device_ids=true | all-gather | bytes 163840 | tf_op jit(solution)/shard_map/all_gather | solution.py:18
  42.1 18.4 %gather_fusion = f32[4096,1024]{1,0:T(8,128)} fusion(f32[64,1024]{1,0:T(8,128)S(1)} %copy.33, s32[4096]{0:T(1024)S(1)} %broadcast_clamp_fusion), kind=kCustom, calls=%fused_computation | custom fusion | bytes 33570816 | tf_op jit(solution)/shard_map/gather | solution.py:52
  60.6 30.5 %copy.34 = f32[64,64,1024]{1,0,2:T(8,128)} copy(f32[64,64,1024]{2,1,0:T(8,128)} %bitcast.59) | data formatting | bytes 33554432 | tf_op jit(solution)/shard_map/gather | solution.py:52
  91.1 1.9 maximum_convert_fusion
  93.9 1.6 copy-done.1
  96.4 6.0 %fusion.26 = f32[4,1024,8]{2,0,1:T(4,128)} fusion(bf16[4,64,1024]{1,0,2:T(4,128)(2,1)S(1)} %copy.35, f32[64]{0:T(128)S(1)} %iota_subtract_fusion, f32[1024,8]{1,0:T(8,128)S(1)} %copy.32), kind=kOutput, calls=%fused_computation.38 | convolution fusion | flops 25690112 | bytes 688384 | tf_op jit(solution)/shard_map/nsc,scm->ncm/dot_general | solution.py:56
  102.4 1.9 copy.37
  104.3 2.5 while.27
  106.9 15.5 %all-gather = f32[4096,8]{0,1:T(8,128)S(1)} all-gather(f32[1024,8]{0,1:T(8,128)S(1)} %get-tuple-element.125), channel_id=2, replica_groups=mesh['groups'=2,'ctx'=4,'mp'=4] {'ctx'}, dimensions={0}, use_global_device_ids=true | all-gather | bytes 163840 | tf_op jit(solution)/shard_map/all_gather | solution.py:18
  123.5 2.5 copy.38
  126.0 10.4 %fusion.8 = f32[1024,64,4]{1,2,0:T(4,128)S(1)} fusion(f32[64]{0:T(128)S(1)} %iota_add_fusion, f32[1024,8]{1,0:T(8,128)S(1)} %copy.32, f32[1024,8]{1,0:T(8,128)S(1)} %copy-done.3, f32[1024,8]{1,0:T(8,128)} %copy.40, f32[4]{0:T(128)S(1)} %iota_multiply_fusion), kind=kOutput, calls=%fused_computation.16 | convolution fusion | flops 26279936 | bytes 1147152 | tf_op jit(solution)/shard_map/ncm,tcm->ntc/dot_general | solution.py:41
  136.5 9.8 %fusion.9 = f32[1024,64,4]{1,2,0:T(4,128)S(1)} fusion(f32[4,1024,8]{2,0,1:T(4,128)S(1)} %copy-done.4, f32[64]{0:T(128)S(1)} %iota_add_fusion, f32[1024,8]{1,0:T(8,128)S(1)} %copy.32, f32[1024,8]{1,0:T(8,128)S(1)} %copy-done.3), kind=kOutput, calls=%fused_computation.17 | convolution fusion | flops 26214400 | bytes 1245440 | tf_op jit(solution)/shard_map/ncm,tcm->ntc/dot_general | solution.py:41
  146.2 29.9 %fusion.12 = bf16[4,64,1024]{1,0,2:T(4,128)(2,1)S(1)} fusion(f32[1024,64,4]{1,2,0:T(4,128)S(1)} %fusion.8, f32[1024,64,4]{1,2,0:T(4,128)S(1)} %fusion.9, bf16[4,64,1024]{1,0,2:T(4,128)(2,1)S(1)} %copy.35, f32[64,64,1024]{1,0,2:T(8,128)} %copy.34, pred[64,64]{1,0:T(8,128)(4,1)S(1)} %subtract_compare_fusion), kind=kOutput, calls=%fused_computation.25 | convolution fusion | flops 206307328 | bytes 19927040 | tf_op jit(solution)/shard_map/tsc,nsc->ntc/dot_general | solution.py:54
  178.1 7.6 %fusion.33 = f32[256,4096]{1,0:T(8,128)} fusion(bf16[1024,4096]{1,0:T(8,128)(2,1)} %all-gather.5.cloned.1.call-done, bf16[256,1024]{1,0:T(8,128)(2,1)S(1)} %bitcast.60, bf16[256,1024]{1,0:T(8,128)(2,1)S(1)} %fusion.35), kind=kOutput, calls=%fused_computation.49 | convolution fusion | flops 2148532224 | bytes 13631488 | tf_op jit(solution)/shard_map/dot_general | solution.py:100
  185.8 46.4 %reduce-scatter.2.cloned.1.call-done = f32[256,1024]{1,0:T(8,128)} async-done(((f32[256,4096]{1,0:T(8,128)}), f32[256,1024]{1,0:T(8,128)}) %reduce-scatter.2.cloned.1.call-update) | async-done | bytes 1048592 | tf_op jit(solution)/shard_map/reduce_scatter | solution.py:105
  232.2 1.4 multiply_reduce_fusion.1
  233.6 5.8 %psum.14 = f32[256]{0:T(256)S(1)} all-reduce(f32[256]{0:T(256)S(1)} %multiply_reduce_fusion.1), channel_id=1, replica_groups=mesh['groups'=2,'ctx'=4,'mp'=4] {'mp'}, use_global_device_ids=true, to_apply=%region_7.8 | all-reduce | flops 256 | bytes 2048 | tf_op jit(solution)/shard_map/psum | solution.py:106
  239.4 2.5 fusion.34
  242.0 23.3 %all-gather.7.cloned.1.call-done = f32[1024,512]{1,0:T(8,128)} async-done(((f32[256,512]{1,0:T(8,128)}), f32[1024,512]{1,0:T(8,128)}) %all-gather.7.cloned.1.call-update) | async-done | bytes 2097168 | tf_op jit(solution)/shard_map/all_gather | solution.py:112
  265.3 1.9 reduce_sum.56
  268.6 1.9 gather_fusion.2
  270.8 12.2 %psum.15 = f32[256]{0:T(256)} all-reduce(f32[256]{0:T(256)S(1)} %and_select_fusion), channel_id=1, replica_groups=mesh['groups'=2,'ctx'=4,'mp'=4] {'ctx'}, use_global_device_ids=true, to_apply=%region_13.14 | all-reduce | flops 256 | bytes 2048 | tf_op jit(solution)/shard_map/psum | solution.py:121
  (73 shorter events, 12.8 us)
Async XLA Ops:
  7.2 232.2 %copy-start = (bf16[1024,512]{1,0:T(8,128)(2,1)S(1)}, bf16[1024,512]{1,0:T(8,128)(2,1)}, u32[]{:S(2)}) copy-start(bf16[1024,512]{1,0:T(8,128)(2,1)} %param.18) | copy-start | bytes 3145732
  7.2 7.9 %copy-start.5 = (f32[3,3,1024]{2,1,0:T(4,128)S(1)}, f32[3,3,1024]{2,1,0:T(4,128)}, u32[]{:S(2)}) copy-start(f32[3,3,1024]{2,1,0:T(4,128)} %param.14) | copy-start | bytes 110596
  7.2 170.9 %all-gather.5.cloned.1.call-start = ((), (), s32[]{:S(2)}) async-start(), calls=%async_computation.1 | async-start | bytes 10485760 | tf_op jit(solution)/shard_map/all_gather | solution.py:102
  7.9 224.3 %reduce-scatter.2.cloned.1.call-start = ((), (), s32[]{:S(2)}) async-start(), calls=%async_computation.2 | async-start | bytes 5242880 | tf_op jit(solution)/shard_map/reduce_scatter | solution.py:105
  8.8 82.3 %collective-permute-start = (bf16[3,2,1024]{2,1,0:T(2,128)(2,1)S(1)}, bf16[3,2,1024]{2,1,0:T(2,128)(2,1)S(1)}, u32[]{:S(2)}, u32[]{:S(2)}) collective-permute-start(bf16[3,2,1024]{2,1,0:T(2,128)(2,1)S(1)} %slice.38), channel_id=1, source_target_pairs={{0,4},{4,8},{8,12},{1,5},{5,9},{9,13},{2,6},{6,10},{10,14},{3,7},{... | collective-permute-start | bytes 36872 | tf_op jit(solution)/shard_map/ppermute | solution.py:13
  15.0 27.0 %copy-start.2 = (f32[1024,8]{1,0:T(8,128)}, f32[1024,8]{1,0:T(8,128)S(1)}, u32[]{:S(2)}) copy-start(f32[1024,8]{1,0:T(8,128)S(1)} %copy.31) | copy-start | bytes 98308
  93.9 1.6 copy-start.1
  102.4 23.6 %copy-start.3 = (f32[1024,8]{1,0:T(8,128)S(1)}, f32[1024,8]{1,0:T(8,128)}, u32[]{:S(2)}) copy-start(f32[1024,8]{1,0:T(8,128)} %copy-done.2) | copy-start | bytes 98308
  126.0 10.4 %copy-start.4 = (f32[4,1024,8]{2,0,1:T(4,128)S(1)}, f32[4,1024,8]{2,0,1:T(4,128)}, u32[]{:S(2)}) copy-start(f32[4,1024,8]{2,0,1:T(4,128)} %copy.38) | copy-start | bytes 393220
  185.7 53.7 %copy-start.6 = (f32[1024]{0:T(1024)S(1)}, f32[1024]{0:T(1024)}, u32[]{:S(2)}) copy-start(f32[1024]{0:T(1024)} %param.17) | copy-start | bytes 12292
  185.7 56.2 %copy-start.7 = (s32[256]{0:T(256)S(1)}, s32[256]{0:T(256)}, u32[]{:S(2)}) copy-start(s32[256]{0:T(256)} %param.20) | copy-start | bytes 3076
  185.8 79.5 %all-gather.7.cloned.1.call-start = ((), (), s32[]{:S(2)}) async-start(), calls=%async_computation.3 | async-start | bytes 2621440 | tf_op jit(solution)/shard_map/all_gather | solution.py:112
  267.2 1.1 copy-start.8
  267.2 3.4 %copy-start.9 = (s32[256]{0:T(256)S(1)}, s32[256]{0:T(256)}, u32[]{:S(2)}) copy-start(s32[256]{0:T(256)} %param.21) | copy-start | bytes 3076
Sparse Core Ops, SparseCore 0:
  9.6 156.0 all-gather.4
  185.9 46.3 reduce-scatter.1
  242.1 23.1 all-gather.6
